TPU v7x, 32 devices: a whole 2x2x4 slice. The times are simulated.
32 devices in a mesh: blk: 16 (over z, x, core), sub: 2 (over y).
Axes of the slice: x: 2, y: 2, z: 4, core: 2. Of those that a mesh axis runs over, the one named last changes fastest.
Arguments:
- vectors: bfloat16 [16, 131072], P('sub', 'blk')
- energies: float32 [131072], P('blk'), may hold values from 1 to 4
- tile_values: bfloat16 [16, 128, 128, 128], P('blk', 'sub'), may hold values from -0.1875 to 0.1875
- tile_rows: int32 [16, 128], P('blk', 'sub'), may hold values from 0 to 63
- tile_cols: int32 [16, 128], P('blk', 'sub'), may hold values from 0 to 63
- tile_offsets: int32 [16, 128], P('blk', 'sub'), may hold values from 0 to 2, as said below
- tile_count: int32 [16, 2], P('blk', 'sub'), may hold values from 8 to 64, as said below
Outputs:
- residual: float32 [16, 131072], P('sub', 'blk')
Inputs may be any that keep to these rules, and one draw needn't show every extreme that they name: `tile_offsets`: an offset never exceeds the row block's index b; where the offset is 0, tile_rows >= tile_cols. `tile_count`: each count is 64 divided by 1, 2, 4 or 8.
All inputs are finite; a program needn't handle non-finite values.
Results may differ from a plain program's by a relative error of at most 0.0003.
Values may be sent and summed in bfloat16 or wider, within the bound.
No kernel may reach another device: no remote copies, remote signals or barrier semaphores. Data moves between devices by JAX's collectives and lax.ppermute only.
A program may use at most 64 MiB of HBM per device.

v0:
```python
import jax
import jax.numpy as jnp
from jax import lax
from jax.sharding import PartitionSpec as P

BW = 2


def from_behind(value, axis, steps):
    count = lax.axis_size(axis)
    first, last = (max(0, -steps), min(count, count - steps))
    return lax.ppermute(value, axis, [(source, source + steps) for source in range(first, last)])


def ritz_coefficients(gram, projected):
    lower = jnp.linalg.cholesky(gram)
    half = lax.linalg.triangular_solve(lower, projected, left_side=True, lower=True)
    return lax.linalg.triangular_solve(lower, half, left_side=True, lower=True, transpose_a=True)


def tile_products(tile_vals, row_ids, col_ids, offset_ids, live, stacked, own_block):
    width, rows_dev = own_block.shape
    tile_side = tile_vals.shape[-1]
    row_tiles = rows_dev // tile_side
    depth = stacked.shape[0]
    highest = lax.Precision.HIGHEST
    grid_view = stacked.reshape(depth, width, row_tiles, tile_side)
    sources = grid_view[offset_ids, :, col_ids, :]
    direct_terms = jnp.einsum(
        "tij,tcj->tci", tile_vals, sources, preferred_element_type=jnp.float32
    )
    own_tiles = own_block.reshape(width, row_tiles, tile_side)[:, row_ids, :]
    mirror_terms = jnp.einsum(
        "tji,ctj->tci", tile_vals, own_tiles, preferred_element_type=jnp.float32
    )
    tile_range = jnp.arange(row_tiles, dtype=jnp.int32)
    row_hot = (row_ids[:, None] == tile_range[None, :]).astype(jnp.float32) * live[:, None]
    col_hot = (col_ids[:, None] == tile_range[None, :]).astype(jnp.float32) * live[:, None]
    depth_hot = (offset_ids[:, None] == jnp.arange(depth, dtype=jnp.int32)[None, :]).astype(
        jnp.float32
    )
    direct = jnp.einsum("tci,tr->cri", direct_terms, row_hot, precision=highest).reshape(
        width, rows_dev
    )
    mirror = jnp.einsum("tci,tk,tr->kcri", mirror_terms, depth_hot, col_hot, precision=highest)
    return (direct, mirror.reshape(depth, width, rows_dev))


def send_back(pieces):
    gathered_sum = pieces[0]
    for offset in range(1, BW + 1):
        gathered_sum = gathered_sum + from_behind(pieces[offset], "blk", -offset)
    return gathered_sum


def on_device(vectors, energies, tile_values, tile_rows, tile_cols, tile_offsets, tile_count):
    columns = vectors.shape[0]
    part_index = lax.axis_index("sub")
    tile_vals = tile_values[0]
    row_ids = tile_rows[0]
    col_ids = tile_cols[0]
    offset_ids = tile_offsets[0]
    live_count = tile_count[0, 0]
    slots = tile_vals.shape[0]
    whole = lax.all_gather(vectors, "sub", axis=0, tiled=True)
    lowered = [whole]
    for offset in range(1, BW + 1):
        lowered.append(from_behind(whole, "blk", offset))
    stacked = jnp.stack(lowered, 0)
    own_block = stacked[0]
    width, rows_dev = own_block.shape
    live = (jnp.arange(slots, dtype=jnp.int32) < live_count).astype(jnp.float32)
    direct, mirror = tile_products(
        tile_vals, row_ids, col_ids, offset_ids, live, stacked, own_block
    )
    mirror = mirror.at[0].add(direct)
    applied = lax.psum_scatter(send_back(mirror), "sub", scatter_dimension=0, tiled=True)
    applied = applied + energies[None, :] * vectors.astype(jnp.float32)
    highest = lax.Precision.HIGHEST
    own_wide = own_block.astype(jnp.float32)
    gram_part = jnp.dot(own_block, vectors.T, preferred_element_type=jnp.float32)
    proj_part = jnp.dot(own_wide, applied.T, precision=highest)
    empty = jnp.zeros((width, width), jnp.float32)
    gram_full = lax.dynamic_update_slice(empty, gram_part, (0, part_index * columns))
    proj_full = lax.dynamic_update_slice(empty, proj_part, (0, part_index * columns))
    gram, projected = lax.psum((gram_full, proj_full), ("blk", "sub"))
    coefficients = ritz_coefficients(gram, projected)
    mine = lax.dynamic_slice_in_dim(coefficients, part_index * columns, columns, 1)
    return applied - jnp.dot(mine.T, own_wide, precision=highest)


def solution(mesh):
    in_specs = (
        P("sub", "blk"),
        P("blk"),
        P("blk", "sub", None, None),
        P("blk", "sub"),
        P("blk", "sub"),
        P("blk", "sub"),
        P("blk", "sub"),
    )
    out_specs = P("sub", "blk")
    return jax.shard_map(
        on_device, mesh=mesh, in_specs=in_specs, out_specs=out_specs, check_vma=False
    )
```

profile of v0, /device:TPU:0, one launch (start us, length us, event | category | flops | bytes accessed | tf_op | source)
XLA Modules:
  0.0 120.8 jit_solution(16180372393465413950)
XLA Ops:
  6.5 7.5 %all_gather.3 = bf16[16,8192]{1,0:T(8,128)(2,1)S(1)} all-gather(bf16[8,8192]{1,0:T(8,128)(2,1)} %param.9), channel_id=1, replica_groups=mesh['blk'=16,'sub'=2] {'sub'}, dimensions={0}, use_global_device_ids=true | all-gather | bytes 393216 | tf_op jit(solution)/shard_map/all_gather | solution.py:65
  14.1 3.6 %collective-permute-start.1 = (bf16[16,8192]{1,0:T(8,128)(2,1)S(1)}, bf16[16,8192]{1,0:T(8,128)(2,1)S(1)}, u32[]{:S(2)}, u32[]{:S(2)}) collective-permute-start(bf16[16,8192]{1,0:T(8,128)(2,1)S(1)} %all_gather.3), channel_id=1, source_target_pairs={{0,4},{2,6},{4,8},{6,10},{8,12},{10,14},{12,16},{14,18},{16,20},{1... | collective-permute-start | bytes 786440 | tf_op jit(solution)/shard_map/ppermute | solution.py:12
  17.6 1.3 %collective-permute-start = (bf16[16,8192]{1,0:T(8,128)(2,1)S(1)}, bf16[16,8192]{1,0:T(8,128)(2,1)S(1)}, u32[]{:S(2)}, u32[]{:S(2)}) collective-permute-start(bf16[16,8192]{1,0:T(8,128)(2,1)S(1)} %all_gather.3), channel_id=1, source_target_pairs={{0,2},{2,4},{4,6},{6,8},{8,10},{10,12},{12,14},{14,16},{16,18},{18... | collective-permute-start | bytes 786440 | tf_op jit(solution)/shard_map/ppermute | solution.py:12
  19.0 0.7 fusion.30
  19.7 0.7 fusion.29
  21.6 0.7 fusion.2
  22.3 1.4 %convolution_bitcast_fusion = f32[3,16,64,128]{3,2,1,0:T(8,128)S(1)} fusion(f32[64,16,128]{2,1,0:T(8,128)S(1)} %fusion.2, f32[64,3]{0,1:T(4,128)S(1)} %fusion.29, f32[64,64]{0,1:T(8,128)S(1)} %fusion.18), kind=kOutput, calls=%fused_computation.7 | convolution fusion | flops 302002176 | bytes 2114304 | tf_op jit(solution)/shard_map/tci,tk,tr->kcri/dot_general | solution.py:45
  23.9 1.1 copy.43
  25.1 1.3 %collective-permute-start.3 = (f32[16,8192]{1,0:T(8,128)}, f32[16,8192]{1,0:T(8,128)}, u32[]{:S(2)}, u32[]{:S(2)}) collective-permute-start(f32[16,8192]{1,0:T(8,128)} %bitcast.93), channel_id=1, source_target_pairs={{4,0},{6,2},{8,4},{10,6},{12,8},{14,10},{16,12},{18,14},{20,16},{2... | collective-permute-start | bytes 1572872 | tf_op jit(solution)/shard_map/ppermute | solution.py:12
  26.4 1.1 copy.44
  27.5 1.3 %collective-permute-start.2 = (f32[16,8192]{1,0:T(8,128)}, f32[16,8192]{1,0:T(8,128)}, u32[]{:S(2)}, u32[]{:S(2)}) collective-permute-start(f32[16,8192]{1,0:T(8,128)} %bitcast.94), channel_id=1, source_target_pairs={{2,0},{4,2},{6,4},{8,6},{10,8},{12,10},{14,12},{16,14},{18,16},{20... | collective-permute-start | bytes 1572872 | tf_op jit(solution)/shard_map/ppermute | solution.py:12
  29.5 1.0 pad_maximum_fusion
  30.5 1.9 %gather_fusion.1 = bf16[64,16,128]{2,1,0:T(8,128)(2,1)S(1)} fusion(bf16[3,16,64,128]{3,1,2,0:T(8,128)(2,1)} %pad_maximum_fusion, s32[64]{0:T(128)S(1)} %fusion.36), kind=kCustom, calls=%fused_computation.1 | custom fusion | bytes 524800 | tf_op jit(solution)/shard_map/gather | solution.py:28
  32.4 1.2 fusion
  33.6 0.7 fusion.7
  34.3 6.7 %collective-permute-done.3 = f32[16,8192]{1,0:T(8,128)} collective-permute-done((f32[16,8192]{1,0:T(8,128)}, f32[16,8192]{1,0:T(8,128)}, u32[]{:S(2)}, u32[]{:S(2)}) %collective-permute-start.3) | collective-permute-done | bytes 524320 | tf_op jit(solution)/shard_map/ppermute | solution.py:12
  41.0 2.6 %fusion.5 = f32[16,8192]{1,0:T(8,128)} fusion(f32[16,8192]{1,0:T(8,128)} %collective-permute-done.3, f32[16,8192]{1,0:T(8,128)} %collective-permute-done.2, f32[2,8,64,128]{3,2,1,0:T(8,128)S(1)} %bitcast.97, f32[2,8,64,128]{3,2,1,0:T(8,128)S(1)} %bitcast.98), kind=kLoop, calls=%fused_computation.14 | loop fusion | flops 393216 | bytes 2621440 | tf_op jit(solution)/shard_map/add | solution.py:52
  44.1 22.2 %reduce-scatter.2.cloned.1.call-done = f32[8,8192]{1,0:T(8,128)} async-done(((f32[16,8192]{1,0:T(8,128)}), f32[8,8192]{1,0:T(8,128)}) %reduce-scatter.2.cloned.1.call-update) | async-done | bytes 262160 | tf_op jit(solution)/shard_map/reduce_scatter | solution.py:77
  66.3 1.4 %convolution_bitcast_fusion.1 = f32[16,8]{1,0:T(8,128)S(1)} fusion(bf16[16,8192]{1,0:T(8,128)(2,1)S(1)} %all_gather.3, f32[8,8192]{1,0:T(8,128)} %reduce-scatter.2.cloned.1.call-done, bf16[8,8192]{1,0:T(8,128)(2,1)S(1)} %copy-done.1, f32[8192]{0:T(1024)S(1)} %copy-done.2), kind=kOutput, calls=%fused_computation.8 | convolution fusion | flops 12779520 | bytes 688640 | tf_op jit(solution)/shard_map/dot_general | solution.py:82
  67.9 39.6 %all-reduce = (f32[16,16]{1,0:T(8,128)S(1)}, f32[16,16]{1,0:T(8,128)S(1)}) all-reduce(f32[16,16]{1,0:T(8,128)S(1)} %dynamic_update_slice.7, f32[16,16]{1,0:T(8,128)S(1)} %dynamic_update_slice.6), channel_id=1, replica_groups=mesh['blk'=16,'sub'=2] {'blk','sub'}, use_global_device_ids=true, to_apply=%region_4.5 | all-reduce | flops 512 | bytes 4096 | tf_op jit(solution)/shard_map/psum | solution.py:86
  107.6 1.5 %cholesky.15 = f32[16,16]{1,0:T(8,128)S(1)} custom-call(f32[16,16]{1,0:T(8,128)S(1)} %fusion.27), custom_call_target="Cholesky" | custom-call | tf_op jit(solution)/shard_map/jit(cholesky)/cholesky | solution.py:16
  109.7 0.6 fusion.22
  110.3 1.2 %custom-call.8 = f32[1,16,16]{1,2,0:T(8,128)S(1)} custom-call(f32[1,16,16]{2,1,0:T(8,128)S(1)} %fusion.22), custom_call_target="InvertDiagBlocksLowerTriangular" | custom-call | tf_op jit(solution)/shard_map/triangular_solve | solution.py:18
  112.0 1.9 %convolution_subtract_fusion = f32[8,8192]{1,0:T(8,128)} fusion(bf16[16,8192]{1,0:T(8,128)(2,1)S(1)} %all_gather.3, f32[8,8192]{1,0:T(8,128)} %reduce-scatter.2.cloned.1.call-done, bf16[8,8192]{1,0:T(8,128)(2,1)S(1)} %copy-done.1, f32[8192]{0:T(1024)S(1)} %copy-done.2, f32[16,16]{0,1:T(8,128)S(1)} %fusion.23, s32[]{:T(128)S(6)} %select_n.42), kind=kOutput, calls=%fused_computation.2 | convolution fusion | flops 12845056 | bytes 954372 | tf_op jit(solution)/shard_map/dot_general | solution.py:89
  (41 shorter events, 3.4 us)
Async XLA Ops:
  6.5 15.1 %copy-start = (bf16[1,64,128,128]{3,2,1,0:T(8,128)(2,1)S(1)}, bf16[1,64,128,128]{3,2,1,0:T(8,128)(2,1)}, u32[]{:S(2)}) copy-start(bf16[1,64,128,128]{3,2,1,0:T(8,128)(2,1)} %param.11) | copy-start | bytes 6291460
  6.5 15.8 %copy-start.4 = (s32[1,64]{1,0:T(1,128)S(1)}, s32[1,64]{1,0:T(1,128)}, u32[]{:S(2)}) copy-start(s32[1,64]{1,0:T(1,128)} %param.13) | copy-start | bytes 772
  6.5 59.7 %reduce-scatter.2.cloned.1.call-start = ((), (), s32[]{:S(2)}) async-start(), calls=%async_computation.1 | async-start | bytes 786432 | tf_op jit(solution)/shard_map/reduce_scatter | solution.py:77
  14.1 15.0 %collective-permute-start.1 = (bf16[16,8192]{1,0:T(8,128)(2,1)S(1)}, bf16[16,8192]{1,0:T(8,128)(2,1)S(1)}, u32[]{:S(2)}, u32[]{:S(2)}) collective-permute-start(bf16[16,8192]{1,0:T(8,128)(2,1)S(1)} %all_gather.3), channel_id=1, source_target_pairs={{0,4},{2,6},{4,8},{6,10},{8,12},{10,14},{12,16},{14,18},{16,20},{1... | collective-permute-start | bytes 786440 | tf_op jit(solution)/shard_map/ppermute | solution.py:12
  17.6 11.6 %collective-permute-start = (bf16[16,8192]{1,0:T(8,128)(2,1)S(1)}, bf16[16,8192]{1,0:T(8,128)(2,1)S(1)}, u32[]{:S(2)}, u32[]{:S(2)}) collective-permute-start(bf16[16,8192]{1,0:T(8,128)(2,1)S(1)} %all_gather.3), channel_id=1, source_target_pairs={{0,2},{2,4},{4,6},{6,8},{8,10},{10,12},{12,14},{14,16},{16,18},{18... | collective-permute-start | bytes 786440 | tf_op jit(solution)/shard_map/ppermute | solution.py:12
  23.9 5.1 %copy-start.5 = (s32[1,64]{1,0:T(1,128)S(1)}, s32[1,64]{1,0:T(1,128)}, u32[]{:S(2)}) copy-start(s32[1,64]{1,0:T(1,128)} %param.14) | copy-start | bytes 772
  25.1 16.0 %collective-permute-start.3 = (f32[16,8192]{1,0:T(8,128)}, f32[16,8192]{1,0:T(8,128)}, u32[]{:S(2)}, u32[]{:S(2)}) collective-permute-start(f32[16,8192]{1,0:T(8,128)} %bitcast.93), channel_id=1, source_target_pairs={{4,0},{6,2},{8,4},{10,6},{12,8},{14,10},{16,12},{18,14},{20,16},{2... | collective-permute-start | bytes 1572872 | tf_op jit(solution)/shard_map/ppermute | solution.py:12
  27.5 13.6 %collective-permute-start.2 = (f32[16,8192]{1,0:T(8,128)}, f32[16,8192]{1,0:T(8,128)}, u32[]{:S(2)}, u32[]{:S(2)}) collective-permute-start(f32[16,8192]{1,0:T(8,128)} %bitcast.94), channel_id=1, source_target_pairs={{2,0},{4,2},{6,4},{8,6},{10,8},{12,10},{14,12},{16,14},{18,16},{20... | collective-permute-start | bytes 1572872 | tf_op jit(solution)/shard_map/ppermute | solution.py:12
  30.5 3.1 %copy-start.3 = (s32[1,64]{1,0:T(1,128)S(1)}, s32[1,64]{1,0:T(1,128)}, u32[]{:S(2)}) copy-start(s32[1,64]{1,0:T(1,128)} %param.12) | copy-start | bytes 772
  33.6 10.1 %copy-start.1 = (bf16[8,8192]{1,0:T(8,128)(2,1)S(1)}, bf16[8,8192]{1,0:T(8,128)(2,1)}, u32[]{:S(2)}) copy-start(bf16[8,8192]{1,0:T(8,128)(2,1)} %param.9) | copy-start | bytes 393220
  33.6 32.7 %copy-start.2 = (f32[8192]{0:T(1024)S(1)}, f32[8192]{0:T(1024)}, u32[]{:S(2)}) copy-start(f32[8192]{0:T(1024)} %param.10) | copy-start | bytes 98308
Sparse Core Ops, SparseCore 0:
  43.8 22.4 reduce-scatter.1
where the time goes:
time: 121 us
  blocking collectives  47.1 us (39%)
  waiting for transfers between devices  28.9 us (24%)
  between operations  14.3 us (12%)
  other arithmetic  8.95 us (7%)
  matrix products  7.91 us (7%)
  starting transfers between devices  7.45 us (6%)
  local copies, waits for them, and re-layouts  6.15 us (5%)
    psum x1, blocking collectives, on_device(): gram, projected = lax.psum((gram_full, proj_full), ('blk', 'sub'))  39.6 us
    reduce_scatter x1, waiting for transfers between devices, on_device(): lax.psum_scatter(send_back(mirror), 'sub', scatter_dimension=0, tiled=True)  22.2 us
    all_gather x1, blocking collectives, on_device(): whole = lax.all_gather(vectors, 'sub', axis=0, tiled=True)  7.51 us
    ppermute x4, starting transfers between devices, from_behind(): lax.ppermute(value, axis, [(source, source + steps) for source in range(f...  7.45 us
    ppermute x4, waiting for transfers between devices, from_behind(): lax.ppermute(value, axis, [(source, source + steps) for source in range(f...  6.71 us
    add x1, other arithmetic, send_back(): gathered_sum = gathered_sum + from_behind(pieces[offset], 'blk', -offset)  2.61 us
  transfers between devices with their start and end apart: 5, of which 2 were waited for; matrix products, arithmetic and copies ran while one was open for 10% of the time, Pallas kernels for 0%

commit v1 on v0

v1 whole, which is shorter than its diff:
```python
import functools

import jax
import jax.numpy as jnp
from jax import lax
from jax.experimental import pallas as pl
from jax.experimental.pallas import tpu as pltpu
from jax.sharding import PartitionSpec as P

BW = 2
GROUP = 8
F32 = jnp.float32
BF16 = jnp.bfloat16
I32 = jnp.int32
HBM = pl.BlockSpec(memory_space=pltpu.HBM)
VMEM = pl.BlockSpec(memory_space=pltpu.VMEM)
SMEM = pl.BlockSpec(memory_space=pltpu.SMEM)
NT = (((1,), (1,)), ((), ()))


def shifted(value, steps):
    count = lax.axis_size("blk")
    first, last = (max(0, -steps), min(count, count - steps))
    return lax.ppermute(value, "blk", [(source, source + steps) for source in range(first, last)])


def swap_sub(value):
    return lax.ppermute(value, "sub", [(0, 1), (1, 0)])


def swap_core(value):
    return lax.ppermute(value, "blk", [(i, i ^ 1) for i in range(lax.axis_size("blk"))])


def rounds_over(axis):
    count = lax.axis_size(axis)
    rounds, stride = [], 1
    while stride < count:
        rest = count // stride
        radix = next(p for p in range(2, rest + 1) if rest % p == 0)
        rounds.append((axis, stride, radix))
        stride *= radix
    return rounds


def run_rounds(value, rounds):
    for axis, stride, radix in rounds:
        total = value
        for turn in range(1, radix):
            pairs = []
            for source in range(lax.axis_size(axis)):
                digit = (source // stride) % radix
                pairs.append((source, source + ((digit + turn) % radix - digit) * stride))
            total = total + lax.ppermute(value, axis, pairs)
        value = total
    return value


def tile_at(index, side):
    return pl.ds(pl.multiple_of(index * side, side), side)


def split2(value):
    spread = value * 65537.0
    high = spread - (spread - value)
    return high, value - high


def odd_block():
    return lax.rem(lax.axis_index("blk"), 2) == 1


def in_order(own, other, out):
    rows = own.shape[0]
    first = lax.axis_index("sub") == 0

    @pl.when(first)
    def _():
        out[0:rows, :] = own[...]
        out[rows : 2 * rows, :] = other[...]

    @pl.when(jnp.logical_not(first))
    def _():
        out[0:rows, :] = other[...]
        out[rows : 2 * rows, :] = own[...]


def load_kernel(source, target, sem):
    copy = pltpu.make_async_copy(source, target, sem)
    copy.start()
    copy.wait()


def join_kernel(own, other, below, out):
    in_order(own, other, out)


def join_below_kernel(own, other, whole, term, out, across, later):
    in_order(own, other, out)
    later[...] = term[...]
    odd = odd_block()

    @pl.when(odd)
    def _():
        across[...] = out[...]

    @pl.when(jnp.logical_not(odd))
    def _():
        across[...] = whole[...]


def levels_at(energies, start, step):
    side = energies.shape[1]
    rows = [energies[pl.ds((start + i) // side, 1), :] for i in range(0, step, side)]
    return jnp.concatenate(rows, 1)


def mirror_kernel(table, vec, energies, tiles, m0, m1, m2, small, acc):
    side = tiles.shape[-1]
    width, rows_dev = vec.shape
    acc[...] = jnp.zeros_like(acc)

    @pl.loop(0, table[3, 0] // GROUP)
    def _(group):
        for lane in range(GROUP):
            slot = group * GROUP + lane
            term = jnp.dot(
                vec[:, tile_at(table[0, slot], side)], tiles[slot], preferred_element_type=F32
            )
            acc[table[2, slot], :, tile_at(table[1, slot], side)] += term

    m0[...] = acc[0]
    m1[...] = acc[1]
    m2[...] = acc[2]
    total = jnp.zeros((width, 3 * width), F32)
    step = 2 * side
    for start in range(0, rows_dev, step):
        v = vec[:, pl.ds(start, step)]
        scaled = split2(levels_at(energies, start, step) * v.astype(F32))
        total += lax.dot_general(
            v,
            jnp.concatenate([v] + [part.astype(BF16) for part in scaled], 0),
            NT,
            preferred_element_type=F32,
        )
    total *= 1.0 / lax.axis_size("sub")
    small[0:width, 0:width] = total[:, :width]
    small[width : 2 * width, 0:width] = total[:, width : 2 * width] + total[:, 2 * width :]


def write_parts(columns, value, targets):
    if len(targets) == 1:
        targets[0][...] = value(slice(None))
        return
    mine = lax.axis_index("sub") * columns
    for start, target in zip((mine, columns - mine), targets):
        target[...] = value(pl.ds(pl.multiple_of(start, columns), columns))


def up_kernel(columns, m2, crossed, *targets):
    odd = odd_block()

    @pl.when(odd)
    def _():
        write_parts(columns, lambda rows: m2[rows, :] + crossed[rows, :], targets)

    @pl.when(jnp.logical_not(odd))
    def _():
        write_parts(columns, lambda rows: m2[rows, :], targets)


def sum_kernel(first, second, small, out, later):
    out[...] = first[...] + second[...]
    later[...] = small[...]


def direct_kernel(
    columns, table, vec, vec1, vec2, tiles, m0, crossed, before, *rest
):
    targets, (small, sources, own) = rest[:-3], rest[-3:]
    side = tiles.shape[-1]
    width, rows_dev = vec.shape
    own[...] = jnp.zeros_like(own)
    sources[0] = vec[...]
    sources[1] = vec1[...]
    sources[2] = vec2[...]

    @pl.loop(0, table[3, 0] // GROUP)
    def _(group):
        for lane in range(GROUP):
            slot = group * GROUP + lane
            term = lax.dot_general(
                sources[table[2, slot], :, tile_at(table[1, slot], side)],
                tiles[slot],
                NT,
                preferred_element_type=F32,
            )
            own[:, tile_at(table[0, slot], side)] += term

    left = jnp.zeros((width, 2 * width), F32)
    right = jnp.zeros((2 * width, width), F32)
    step = 2 * side
    for start in range(0, rows_dev, step):
        here = pl.ds(start, step)
        v = vec[:, here]
        parts = jnp.concatenate([part.astype(BF16) for part in split2(own[:, here])], 0)
        left += lax.dot_general(v, parts, NT, preferred_element_type=F32)
        right += lax.dot_general(parts, v, NT, preferred_element_type=F32)
    small[0:width, 0:width] = before[0:width, 0:width]
    small[width : 2 * width, 0:width] = before[width : 2 * width, 0:width] + (
        (left[:, :width] + left[:, width:]) + (right[:width] + right[width:])
    )
    odd = odd_block()

    @pl.when(odd)
    def _():
        write_parts(columns, lambda part: own[part, :] + m0[part, :], targets)

    @pl.when(jnp.logical_not(odd))
    def _():
        write_parts(
            columns, lambda part: own[part, :] + (m0[part, :] + crossed[part, :]), targets
        )


def eliminate(system):
    width = system.shape[1]
    col_id = lax.broadcasted_iota(I32, system.shape, 1)
    for pivot in range(width):
        column = system[:, pivot : pivot + 1] / system[pivot : pivot + 1, pivot : pivot + 1]
        row = system[pivot : pivot + 1, :]
        system = jnp.where(col_id == pivot, column, system - column * row)
    return system[width:, :]


def final_kernel(small, vec, mine, energies, *rest):
    terms, (out, coeffs) = rest[:-2], rest[-2:]
    width, rows_dev = vec.shape
    columns = mine.shape[0]
    side = energies.shape[1]
    coeffs[...] = eliminate(small[:, :width])
    wanted = coeffs[pl.ds(lax.axis_index("sub") * columns, columns), :]
    high, rest_of = split2(wanted)
    mid, low = split2(rest_of)
    factors = jnp.concatenate([high, mid, low], 0).astype(BF16)
    step = 8 * side
    for start in range(0, rows_dev, step):
        here = pl.ds(start, step)
        model = jnp.dot(factors, vec[:, here], preferred_element_type=F32)
        model = model[:columns] + (model[columns : 2 * columns] + model[2 * columns :])
        applied = levels_at(energies, start, step) * mine[:, here].astype(F32)
        for term in terms:
            applied = applied + term[:, here]
        out[:, here] = applied - model


def call(kernel, name, out_shape, in_specs, out_specs, args, cycles, scratch=(), room=24):
    return pl.pallas_call(
        kernel,
        out_shape=out_shape,
        in_specs=in_specs,
        out_specs=out_specs,
        scratch_shapes=list(scratch),
        compiler_params=pltpu.CompilerParams(vmem_limit_bytes=room * 1024 * 1024),
        cost_estimate=pl.CostEstimate(
            flops=0, bytes_accessed=cycles * 3_000_000, transcendentals=0
        ),
        name=name,
    )(*args)


def on_device(vectors, energies, tile_values, tile_rows, tile_cols, tile_offsets, tile_count):
    columns, rows_dev = vectors.shape
    n_sub = lax.axis_size("sub")
    pair = n_sub == 2
    width = columns * n_sub
    slots, side = tile_values.shape[1:3]
    levels = energies.reshape(rows_dev // side, side)
    narrow = jax.ShapeDtypeStruct((width, rows_dev), BF16)
    block = jax.ShapeDtypeStruct((width, rows_dev), F32)
    half = jax.ShapeDtypeStruct((columns, rows_dev), F32)
    square = jax.ShapeDtypeStruct((2 * width, side), F32)
    parts = [half] * 2 if pair else [block]

    table = jnp.concatenate(
        [tile_rows, tile_cols, tile_offsets, jnp.broadcast_to(tile_count, tile_rows.shape)], 0
    )
    tiles = call(
        load_kernel,
        "load",
        jax.ShapeDtypeStruct((slots, side, side), BF16),
        [HBM],
        VMEM,
        (tile_values.reshape(slots, side, side),),
        1,
        [pltpu.SemaphoreType.DMA],
        60,
    )
    if pair:
        other = swap_sub(vectors)
        below = shifted(vectors, BW)
        whole = call(join_kernel, "join", narrow, [VMEM] * 3, VMEM, (vectors, other, below), 1)
    else:
        whole = lax.all_gather(vectors, "sub", axis=0, tiled=True)
    m0, m1, m2, before = call(
        mirror_kernel,
        "mirror",
        [block] * 3 + [square],
        [SMEM] + [VMEM] * 3,
        [VMEM] * 4,
        (table, whole, levels, tiles),
        2,
        [pltpu.VMEM((BW + 1, width, rows_dev), F32)],
    )
    if pair:
        whole2, across, m1 = call(
            join_below_kernel,
            "join_below",
            [narrow] * 2 + [block],
            [VMEM] * 4,
            [VMEM] * 3,
            (below, swap_sub(below), whole, m1),
            1,
        )
    else:
        whole2 = shifted(whole, BW)
        across = jnp.where(lax.rem(lax.axis_index("blk"), 2) == 1, whole2, whole)
    whole1 = swap_core(across)
    crossed = swap_core(m1)
    up = call(
        functools.partial(up_kernel, columns),
        "up",
        parts,
        [VMEM] * 2,
        [VMEM] * len(parts),
        (m2, crossed),
        1,
    )
    *own, small = call(
        functools.partial(direct_kernel, columns),
        "direct",
        parts + [square],
        [SMEM] + [VMEM] * 7,
        [VMEM] * (len(parts) + 1),
        (table, whole, whole1, whole2, tiles, m0, crossed, before),
        3,
        [pltpu.VMEM((BW + 1, width, rows_dev), BF16), pltpu.VMEM((width, rows_dev), F32)],
    )
    rounds = rounds_over("blk")
    small = run_rounds(small, rounds[:2])
    if pair:
        up, small = call(
            sum_kernel,
            "sum",
            [half, square],
            [VMEM] * 3,
            [VMEM] * 2,
            (up[0], swap_sub(up[1]), small),
            1,
        )
        terms = [own[0], swap_sub(own[1])]
    else:
        up = lax.psum_scatter(up[0], "sub", scatter_dimension=0, tiled=True)
        terms = [lax.psum_scatter(own[0], "sub", scatter_dimension=0, tiled=True)]
    terms.append(shifted(up, -BW))
    small = run_rounds(small, rounds_over("sub") + rounds[2:])
    return call(
        final_kernel,
        "final",
        half,
        [VMEM] * (4 + len(terms)),
        VMEM,
        (small, whole, vectors, levels, *terms),
        2,
        [pltpu.VMEM((width, width), F32)],
    )


def solution(mesh):
    in_specs = (
        P("sub", "blk"),
        P("blk"),
        P("blk", "sub", None, None),
        P("blk", "sub"),
        P("blk", "sub"),
        P("blk", "sub"),
        P("blk", "sub"),
    )
    out_specs = P("sub", "blk")
    return jax.shard_map(
        on_device, mesh=mesh, in_specs=in_specs, out_specs=out_specs, check_vma=False
    )
```

time: 121 us -> 44.7 us (0.37)
  blocking collectives: 47.1 us -> 0 us
  waiting for transfers between devices: 28.9 us -> 12.7 us
  between operations: 14.3 us -> 0.81 us
  Pallas kernels: 0 us -> 11.5 us
  starting transfers between devices: 7.45 us -> 17.9 us
  other arithmetic: 8.95 us -> 0.09 us
  matrix products: 7.91 us -> 0 us
  local copies, waits for them, and re-layouts: 6.15 us -> 1.68 us
    psum x1 -> x0, blocking collectives: 39.6 us -> none  [on_device(): gram, projected = lax.psum((gram_full, proj_full), ('blk', 'sub'))]
    reduce_scatter x1 -> x0, waiting for transfers between devices: 22.2 us -> none  [on_device(): lax.psum_scatter(send_back(mirror), 'sub', scatter_dimension=0, tiled=True)]
    pallas_call x0 -> x8, Pallas kernels: none -> 11.5 us  [call(): pl.pallas_call(kernel, out_shape=out_shape, in_specs=in_specs, out_specs=...]
    ppermute x4 -> x13, starting transfers between devices: 7.45 us -> 17.9 us  [the longest x5 8.04 us: run_rounds(): total = total + lax.ppermute(value, axis, pairs)]
    all_gather x1 -> x0, blocking collectives: 7.51 us -> none  [on_device(): whole = lax.all_gather(vectors, 'sub', axis=0, tiled=True)]
    dot_general x7 -> x0, matrix products: 7.5 us -> none  [the longest x1 1.92 us: on_device(): return applied - jnp.dot(mine.T, own_wide, precision=highest)]
    ppermute x4 -> x13, waiting for transfers between devices: 6.71 us -> 12.7 us  [the longest x5 11.2 us: run_rounds(): total = total + lax.ppermute(value, axis, pairs)]
    another operation x7 -> x0, other arithmetic: 5.64 us -> none  [the longest x3 2.13 us: ritz_coefficients(): lower = jnp.linalg.cholesky(gram)]
  transfers between devices with their start and end apart: 5 -> 13, of which waited for: 2 -> 6; matrix products, arithmetic and copies ran while one was open for 10% -> 0% of each run, Pallas kernels for 0% -> 20%
where the time goes in v1:
time: 44.7 us; the launch traced here: 44.6 us
  starting transfers between devices  17.9 us (40%)
  waiting for transfers between devices  12.7 us (28%)
  Pallas kernels  11.5 us (26%)
  local copies, waits for them, and re-layouts  1.68 us (4%)
  between operations  0.81 us (2%)
    pallas_call x8, Pallas kernels, call(): pl.pallas_call(kernel, out_shape=out_shape, in_specs=in_specs, out_specs=...  11.5 us
    ppermute x5, waiting for transfers between devices, run_rounds(): total = total + lax.ppermute(value, axis, pairs)  11.2 us
    ppermute x5, starting transfers between devices, run_rounds(): total = total + lax.ppermute(value, axis, pairs)  8.04 us
    ppermute x2, starting transfers between devices, shifted(): lax.ppermute(value, 'blk', [(source, source + steps) for source in range(...  6.13 us
    ppermute x4, starting transfers between devices, swap_sub(): return lax.ppermute(value, 'sub', [(0, 1), (1, 0)])  3.17 us
    unnamed x14, local copies, waits for them, and re-layouts  1.61 us
    ppermute x2, waiting for transfers between devices, swap_core(): lax.ppermute(value, 'blk', [(i, i ^ 1) for i in range(lax.axis_size('blk'...  1.4 us
  transfers between devices with their start and end apart: 13, of which 6 were waited for; matrix products, arithmetic and copies ran while one was open for 0% of the time, Pallas kernels for 20%

profile of v1, /device:TPU:0, one launch (start us, length us, event | category | flops | bytes accessed | tf_op | source)
XLA Modules:
  0.0 44.6 jit_solution(15247659235384477364)
XLA Ops:
  0.0 4.8 %collective-permute-start.1 = (bf16[8,8192]{1,0:T(8,128)(2,1)}, bf16[8,8192]{1,0:T(8,128)(2,1)S(1)}, u32[]{:S(2)}, u32[]{:S(2)}) collective-permute-start(bf16[8,8192]{1,0:T(8,128)(2,1)} %mine.1), channel_id=1, source_target_pairs={{0,4},{2,6},{4,8},{6,10},{8,12},{10,14},{12,16},{14,18},{16,20},{1... | collective-permute-start | bytes 393224 | tf_op jit(solution)/shard_map/ppermute | solution.py:24
  4.8 1.6 %collective-permute-start = (bf16[8,8192]{1,0:T(8,128)(2,1)}, bf16[8,8192]{1,0:T(8,128)(2,1)S(1)}, u32[]{:S(2)}, u32[]{:S(2)}) collective-permute-start(bf16[8,8192]{1,0:T(8,128)(2,1)} %mine.1), channel_id=1, source_target_pairs={{0,1},{1,0},{2,3},{3,2},{4,5},{5,4},{6,7},{7,6},{8,9},{9,8},{10,11... | collective-permute-start | bytes 393224 | tf_op jit(solution)/shard_map/ppermute | solution.py:28
  7.1 3.0 %load.1.tiles = bf16[64,128,128]{2,1,0:T(8,128)(2,1)} custom-call(bf16[64,128,128]{2,1,0:T(8,128)(2,1)} %bitcast.8), custom_call_target="tpu_custom_call" | custom-call | bytes 3000000 | tf_op jit(solution)/shard_map/load/pallas_call | solution.py:258
  10.1 0.1 pad.3.clone
  10.2 0.5 %collective-permute-start.2 = (bf16[8,8192]{1,0:T(8,128)(2,1)S(1)}, bf16[8,8192]{1,0:T(8,128)(2,1)S(1)}, u32[]{:S(2)}, u32[]{:S(2)}) collective-permute-start(bf16[8,8192]{1,0:T(8,128)(2,1)S(1)} %collective-permute-done.1.below.own), channel_id=1, source_target_pairs={{0,1},{1,0},{2,3},{3,2},{4,5},{5,4},{6,7},{7,6},{8,9},{9,8},{10,11... | collective-permute-start | bytes 393224 | tf_op jit(solution)/shard_map/ppermute | solution.py:28
  10.9 1.6 %copy-done = bf16[64,128,128]{2,1,0:T(8,128)(2,1)S(1)} copy-done((bf16[64,128,128]{2,1,0:T(8,128)(2,1)S(1)}, bf16[64,128,128]{2,1,0:T(8,128)(2,1)}, u32[]{:S(2)}) %copy-start) | copy-done | bytes 2097176
  12.4 2.7 %mirror.1 = (f32[16,8192]{1,0:T(8,128)S(1)}, f32[16,8192]{1,0:T(8,128)S(1)}, f32[16,8192]{1,0:T(8,128)S(1)}, f32[32,128]{1,0:T(8,128)S(1)}) custom-call(s32[4,64]{1,0:T(4,128)S(1)} %add_add_fusion.table, bf16[16,8192]{1,0:T(8,128)(2,1)S(1)} %join.1.vec.whole, f32[64,128]{1,0:T(8,128)S(1)} %bitcast.6, bf16[64,128,128]{2,1,0:T(8,128)(2,1)S(1)} %copy-done), custom_call_target="tpu_custom_call" | custom-call | bytes 6000000 | tf_op jit(solution)/shard_map/mirror/pallas_call | solution.py:258
  15.2 0.1 join_below.1
  15.4 0.5 %collective-permute-start.5 = (bf16[16,8192]{1,0:T(8,128)(2,1)S(1)}, bf16[16,8192]{1,0:T(8,128)(2,1)S(1)}, u32[]{:S(2)}, u32[]{:S(2)}) collective-permute-start(bf16[16,8192]{1,0:T(8,128)(2,1)S(1)} %get-tuple-element.24), channel_id=1, source_target_pairs={{0,2},{2,0},{4,6},{6,4},{8,10},{10,8},{12,14},{14,12},{16,18},{18,... | collective-permute-start | bytes 786440 | tf_op jit(solution)/shard_map/ppermute | solution.py:32
  15.9 1.4 %collective-permute-done.3.crossed = f32[16,8192]{1,0:T(8,128)S(1)} collective-permute-done((f32[16,8192]{1,0:T(8,128)S(1)}, f32[16,8192]{1,0:T(8,128)S(1)}, u32[]{:S(2)}, u32[]{:S(2)}) %collective-permute-start.3) | collective-permute-done | bytes 524320 | tf_op jit(solution)/shard_map/ppermute | solution.py:32
  17.3 0.5 %collective-permute-start.4 = (f32[8,8192]{1,0:T(8,128)S(1)}, f32[8,8192]{1,0:T(8,128)S(1)}, u32[]{:S(2)}, u32[]{:S(2)}) collective-permute-start(f32[8,8192]{1,0:T(8,128)S(1)} %get-tuple-element.23), channel_id=1, source_target_pairs={{0,1},{1,0},{2,3},{3,2},{4,5},{5,4},{6,7},{7,6},{8,9},{9,8},{10,11... | collective-permute-start | bytes 786440 | tf_op jit(solution)/shard_map/ppermute | solution.py:28
  17.9 3.3 %direct.1 = (f32[8,8192]{1,0:T(8,128)S(1)}, f32[8,8192]{1,0:T(8,128)S(1)}, f32[32,128]{1,0:T(8,128)S(1)}) custom-call(s32[4,64]{1,0:T(4,128)S(1)} %add_add_fusion.table, bf16[16,8192]{1,0:T(8,128)(2,1)S(1)} %join.1.vec.whole, bf16[16,8192]{1,0:T(8,128)(2,1)S(1)} %collective-permute-done.5.vec1, bf16[16,8192]{1,0:T(8,128)(2,1)S(1)} %get-tuple-element.25.vec2, ...), custom_call_target="tpu_custom_call" | custom-call | bytes 9000000 | tf_op jit(solution)/shard_map/direct/pallas_call | solution.py:258
  21.2 1.2 %collective-permute-done.6 = f32[32,128]{1,0:T(8,128)S(1)} collective-permute-done((f32[32,128]{1,0:T(8,128)S(1)}, f32[32,128]{1,0:T(8,128)S(1)}, u32[]{:S(2)}, u32[]{:S(2)}) %collective-permute-start.6) | collective-permute-done | bytes 16416 | tf_op jit(solution)/shard_map/ppermute | solution.py:54
  22.4 2.6 %collective-permute-start.7 = (f32[32,128]{1,0:T(8,128)S(1)}, f32[32,128]{1,0:T(8,128)S(1)}, u32[]{:S(2)}, u32[]{:S(2)}) collective-permute-start(f32[32,128]{1,0:T(8,128)S(1)} %add.15), channel_id=1, source_target_pairs={{0,4},{2,6},{4,0},{6,2},{8,12},{10,14},{12,8},{14,10},{16,20},{18,... | collective-permute-start | bytes 49160 | tf_op jit(solution)/shard_map/ppermute | solution.py:54
  25.0 0.5 %collective-permute-start.11 = (f32[8,8192]{1,0:T(8,128)S(1)}, f32[8,8192]{1,0:T(8,128)S(1)}, u32[]{:S(2)}, u32[]{:S(2)}) collective-permute-start(f32[8,8192]{1,0:T(8,128)S(1)} %get-tuple-element.31), channel_id=1, source_target_pairs={{0,1},{1,0},{2,3},{3,2},{4,5},{5,4},{6,7},{7,6},{8,9},{9,8},{10,11... | collective-permute-start | bytes 786440 | tf_op jit(solution)/shard_map/ppermute | solution.py:28
  25.5 1.2 %collective-permute-done.7 = f32[32,128]{1,0:T(8,128)S(1)} collective-permute-done((f32[32,128]{1,0:T(8,128)S(1)}, f32[32,128]{1,0:T(8,128)S(1)}, u32[]{:S(2)}, u32[]{:S(2)}) %collective-permute-start.7) | collective-permute-done | bytes 16416 | tf_op jit(solution)/shard_map/ppermute | solution.py:54
  26.7 1.3 %collective-permute-start.12 = (f32[8,8192]{1,0:T(8,128)S(1)}, f32[8,8192]{1,0:T(8,128)S(1)}, u32[]{:S(2)}, u32[]{:S(2)}) collective-permute-start(f32[8,8192]{1,0:T(8,128)S(1)} %get-tuple-element.32), channel_id=1, source_target_pairs={{4,0},{6,2},{8,4},{10,6},{12,8},{14,10},{16,12},{18,14},{20,16},{2... | collective-permute-start | bytes 786440 | tf_op jit(solution)/shard_map/ppermute | solution.py:24
  28.0 0.6 %collective-permute-start.8 = (f32[32,128]{1,0:T(8,128)S(1)}, f32[32,128]{1,0:T(8,128)S(1)}, u32[]{:S(2)}, u32[]{:S(2)}) collective-permute-start(f32[32,128]{1,0:T(8,128)S(1)} %get-tuple-element.29), channel_id=1, source_target_pairs={{0,1},{1,0},{2,3},{3,2},{4,5},{5,4},{6,7},{7,6},{8,9},{9,8},{10,11... | collective-permute-start | bytes 49160 | tf_op jit(solution)/shard_map/ppermute | solution.py:54
  28.6 4.8 %collective-permute-done.8 = f32[32,128]{1,0:T(8,128)S(1)} collective-permute-done((f32[32,128]{1,0:T(8,128)S(1)}, f32[32,128]{1,0:T(8,128)S(1)}, u32[]{:S(2)}, u32[]{:S(2)}) %collective-permute-start.8) | collective-permute-done | bytes 16416 | tf_op jit(solution)/shard_map/ppermute | solution.py:54
  33.4 2.5 %collective-permute-start.9 = (f32[32,128]{1,0:T(8,128)S(1)}, f32[32,128]{1,0:T(8,128)S(1)}, u32[]{:S(2)}, u32[]{:S(2)}) collective-permute-start(f32[32,128]{1,0:T(8,128)S(1)} %add.17), channel_id=1, source_target_pairs={{0,8},{2,10},{4,12},{6,14},{8,0},{10,2},{12,4},{14,6},{16,24},{18,... | collective-permute-start | bytes 49160 | tf_op jit(solution)/shard_map/ppermute | solution.py:54
  35.9 1.7 %collective-permute-done.9 = f32[32,128]{1,0:T(8,128)S(1)} collective-permute-done((f32[32,128]{1,0:T(8,128)S(1)}, f32[32,128]{1,0:T(8,128)S(1)}, u32[]{:S(2)}, u32[]{:S(2)}) %collective-permute-start.9) | collective-permute-done | bytes 16416 | tf_op jit(solution)/shard_map/ppermute | solution.py:54
  37.7 2.3 %collective-permute-start.10 = (f32[32,128]{1,0:T(8,128)S(1)}, f32[32,128]{1,0:T(8,128)S(1)}, u32[]{:S(2)}, u32[]{:S(2)}) collective-permute-start(f32[32,128]{1,0:T(8,128)S(1)} %add.18), channel_id=1, source_target_pairs={{0,16},{2,18},{4,20},{6,22},{8,24},{10,26},{12,28},{14,30},{16,0},... | collective-permute-start | bytes 49160 | tf_op jit(solution)/shard_map/ppermute | solution.py:54
  39.9 2.3 %collective-permute-done.10 = f32[32,128]{1,0:T(8,128)S(1)} collective-permute-done((f32[32,128]{1,0:T(8,128)S(1)}, f32[32,128]{1,0:T(8,128)S(1)}, u32[]{:S(2)}, u32[]{:S(2)}) %collective-permute-start.10) | collective-permute-done | bytes 16416 | tf_op jit(solution)/shard_map/ppermute | solution.py:54
  42.3 2.3 %final.1 = f32[8,8192]{1,0:T(8,128)} custom-call(f32[32,128]{1,0:T(8,128)S(1)} %add.19.small, bf16[16,8192]{1,0:T(8,128)(2,1)S(1)} %join.1.vec.whole, bf16[8,8192]{1,0:T(8,128)(2,1)S(1)} %copy-done.2, f32[64,128]{1,0:T(8,128)S(1)} %bitcast.7, f32[8,8192]{1,0:T(8,128)S(1)} %get-tuple-element.30.rest_0_, f32[8,8192]{1,0:T(8,128)S(1)} %collective-permute-done.11.rest_1_, ...), custom_call_target="tpu_custom_call" | custom-call | bytes 6000000 | tf_op jit(solution)/shard_map/final/pallas_call | solution.py:258
  (31 shorter events, 0.4 us)
Async XLA Ops:
  0.0 10.2 %collective-permute-start.1 = (bf16[8,8192]{1,0:T(8,128)(2,1)}, bf16[8,8192]{1,0:T(8,128)(2,1)S(1)}, u32[]{:S(2)}, u32[]{:S(2)}) collective-permute-start(bf16[8,8192]{1,0:T(8,128)(2,1)} %mine.1), channel_id=1, source_target_pairs={{0,4},{2,6},{4,8},{6,10},{8,12},{10,14},{12,16},{14,18},{16,20},{1... | collective-permute-start | bytes 393224 | tf_op jit(solution)/shard_map/ppermute | solution.py:24
  4.8 6.0 %collective-permute-start = (bf16[8,8192]{1,0:T(8,128)(2,1)}, bf16[8,8192]{1,0:T(8,128)(2,1)S(1)}, u32[]{:S(2)}, u32[]{:S(2)}) collective-permute-start(bf16[8,8192]{1,0:T(8,128)(2,1)} %mine.1), channel_id=1, source_target_pairs={{0,1},{1,0},{2,3},{3,2},{4,5},{5,4},{6,7},{7,6},{8,9},{9,8},{10,11... | collective-permute-start | bytes 393224 | tf_op jit(solution)/shard_map/ppermute | solution.py:28
  7.1 3.6 %copy-start.4 = (s32[1,64]{1,0:T(1,128)S(1)}, s32[1,64]{1,0:T(1,128)}, u32[]{:S(2)}) copy-start(s32[1,64]{1,0:T(1,128)} %param.12) | copy-start | bytes 772
  7.1 3.6 %copy-start.5 = (s32[1,64]{1,0:T(1,128)S(1)}, s32[1,64]{1,0:T(1,128)}, u32[]{:S(2)}) copy-start(s32[1,64]{1,0:T(1,128)} %param.11) | copy-start | bytes 772
  7.1 3.6 %copy-start.6 = (s32[1,64]{1,0:T(1,128)S(1)}, s32[1,64]{1,0:T(1,128)}, u32[]{:S(2)}) copy-start(s32[1,64]{1,0:T(1,128)} %param.10) | copy-start | bytes 772
  7.1 3.7 %copy-start.2 = (bf16[8,8192]{1,0:T(8,128)(2,1)S(1)}, bf16[8,8192]{1,0:T(8,128)(2,1)}, u32[]{:S(2)}) copy-start(bf16[8,8192]{1,0:T(8,128)(2,1)} %mine.1) | copy-start | bytes 393220
  7.1 3.7 %copy-start.3 = (f32[8192]{0:T(1024)S(1)}, f32[8192]{0:T(1024)}, u32[]{:S(2)}) copy-start(f32[8192]{0:T(1024)} %param.8) | copy-start | bytes 98308
  10.2 5.0 %collective-permute-start.2 = (bf16[8,8192]{1,0:T(8,128)(2,1)S(1)}, bf16[8,8192]{1,0:T(8,128)(2,1)S(1)}, u32[]{:S(2)}, u32[]{:S(2)}) collective-permute-start(bf16[8,8192]{1,0:T(8,128)(2,1)S(1)} %collective-permute-done.1.below.own), channel_id=1, source_target_pairs={{0,1},{1,0},{2,3},{3,2},{4,5},{5,4},{6,7},{7,6},{8,9},{9,8},{10,11... | collective-permute-start | bytes 393224 | tf_op jit(solution)/shard_map/ppermute | solution.py:28
  10.8 1.6 %copy-start = (bf16[64,128,128]{2,1,0:T(8,128)(2,1)S(1)}, bf16[64,128,128]{2,1,0:T(8,128)(2,1)}, u32[]{:S(2)}) copy-start(bf16[64,128,128]{2,1,0:T(8,128)(2,1)} %load.1.tiles) | copy-start | bytes 6291460
  12.4 5.4 %copy-start.1 = (bf16[64,128,128]{2,1,0:T(8,128)(2,1)S(1)}, bf16[64,128,128]{2,1,0:T(8,128)(2,1)}, u32[]{:S(2)}) copy-start(bf16[64,128,128]{2,1,0:T(8,128)(2,1)} %load.1.tiles) | copy-start | bytes 6291460
  15.3 2.0 %collective-permute-start.3 = (f32[16,8192]{1,0:T(8,128)S(1)}, f32[16,8192]{1,0:T(8,128)S(1)}, u32[]{:S(2)}, u32[]{:S(2)}) collective-permute-start(f32[16,8192]{1,0:T(8,128)S(1)} %get-tuple-element.21), channel_id=1, source_target_pairs={{0,2},{2,0},{4,6},{6,4},{8,10},{10,8},{12,14},{14,12},{16,18},{18,... | collective-permute-start | bytes 1572872 | tf_op jit(solution)/shard_map/ppermute | solution.py:32
  15.4 2.5 %collective-permute-start.5 = (bf16[16,8192]{1,0:T(8,128)(2,1)S(1)}, bf16[16,8192]{1,0:T(8,128)(2,1)S(1)}, u32[]{:S(2)}, u32[]{:S(2)}) collective-permute-start(bf16[16,8192]{1,0:T(8,128)(2,1)S(1)} %get-tuple-element.24), channel_id=1, source_target_pairs={{0,2},{2,0},{4,6},{6,4},{8,10},{10,8},{12,14},{14,12},{16,18},{18,... | collective-permute-start | bytes 786440 | tf_op jit(solution)/shard_map/ppermute | solution.py:32
  17.3 9.4 %collective-permute-start.4 = (f32[8,8192]{1,0:T(8,128)S(1)}, f32[8,8192]{1,0:T(8,128)S(1)}, u32[]{:S(2)}, u32[]{:S(2)}) collective-permute-start(f32[8,8192]{1,0:T(8,128)S(1)} %get-tuple-element.23), channel_id=1, source_target_pairs={{0,1},{1,0},{2,3},{3,2},{4,5},{5,4},{6,7},{7,6},{8,9},{9,8},{10,11... | collective-permute-start | bytes 786440 | tf_op jit(solution)/shard_map/ppermute | solution.py:28
  21.1 1.2 %collective-permute-start.6 = (f32[32,128]{1,0:T(8,128)S(1)}, f32[32,128]{1,0:T(8,128)S(1)}, u32[]{:S(2)}, u32[]{:S(2)}) collective-permute-start(f32[32,128]{1,0:T(8,128)S(1)} %get-tuple-element.28), channel_id=1, source_target_pairs={{0,2},{2,0},{4,6},{6,4},{8,10},{10,8},{12,14},{14,12},{16,18},{18,... | collective-permute-start | bytes 49160 | tf_op jit(solution)/shard_map/ppermute | solution.py:54
  22.4 4.3 %collective-permute-start.7 = (f32[32,128]{1,0:T(8,128)S(1)}, f32[32,128]{1,0:T(8,128)S(1)}, u32[]{:S(2)}, u32[]{:S(2)}) collective-permute-start(f32[32,128]{1,0:T(8,128)S(1)} %add.15), channel_id=1, source_target_pairs={{0,4},{2,6},{4,0},{6,2},{8,12},{10,14},{12,8},{14,10},{16,20},{18,... | collective-permute-start | bytes 49160 | tf_op jit(solution)/shard_map/ppermute | solution.py:54
  25.0 17.4 %collective-permute-start.11 = (f32[8,8192]{1,0:T(8,128)S(1)}, f32[8,8192]{1,0:T(8,128)S(1)}, u32[]{:S(2)}, u32[]{:S(2)}) collective-permute-start(f32[8,8192]{1,0:T(8,128)S(1)} %get-tuple-element.31), channel_id=1, source_target_pairs={{0,1},{1,0},{2,3},{3,2},{4,5},{5,4},{6,7},{7,6},{8,9},{9,8},{10,11... | collective-permute-start | bytes 786440 | tf_op jit(solution)/shard_map/ppermute | solution.py:28
  26.7 15.6 %collective-permute-start.12 = (f32[8,8192]{1,0:T(8,128)S(1)}, f32[8,8192]{1,0:T(8,128)S(1)}, u32[]{:S(2)}, u32[]{:S(2)}) collective-permute-start(f32[8,8192]{1,0:T(8,128)S(1)} %get-tuple-element.32), channel_id=1, source_target_pairs={{4,0},{6,2},{8,4},{10,6},{12,8},{14,10},{16,12},{18,14},{20,16},{2... | collective-permute-start | bytes 786440 | tf_op jit(solution)/shard_map/ppermute | solution.py:24
  28.0 5.4 %collective-permute-start.8 = (f32[32,128]{1,0:T(8,128)S(1)}, f32[32,128]{1,0:T(8,128)S(1)}, u32[]{:S(2)}, u32[]{:S(2)}) collective-permute-start(f32[32,128]{1,0:T(8,128)S(1)} %get-tuple-element.29), channel_id=1, source_target_pairs={{0,1},{1,0},{2,3},{3,2},{4,5},{5,4},{6,7},{7,6},{8,9},{9,8},{10,11... | collective-permute-start | bytes 49160 | tf_op jit(solution)/shard_map/ppermute | solution.py:54
  33.4 4.2 %collective-permute-start.9 = (f32[32,128]{1,0:T(8,128)S(1)}, f32[32,128]{1,0:T(8,128)S(1)}, u32[]{:S(2)}, u32[]{:S(2)}) collective-permute-start(f32[32,128]{1,0:T(8,128)S(1)} %add.17), channel_id=1, source_target_pairs={{0,8},{2,10},{4,12},{6,14},{8,0},{10,2},{12,4},{14,6},{16,24},{18,... | collective-permute-start | bytes 49160 | tf_op jit(solution)/shard_map/ppermute | solution.py:54
  37.7 4.6 %collective-permute-start.10 = (f32[32,128]{1,0:T(8,128)S(1)}, f32[32,128]{1,0:T(8,128)S(1)}, u32[]{:S(2)}, u32[]{:S(2)}) collective-permute-start(f32[32,128]{1,0:T(8,128)S(1)} %add.18), channel_id=1, source_target_pairs={{0,16},{2,18},{4,20},{6,22},{8,24},{10,26},{12,28},{14,30},{16,0},... | collective-permute-start | bytes 49160 | tf_op jit(solution)/shard_map/ppermute | solution.py:54
